TPU v7x, 32 devices: a whole 2x2x4 slice. The times are simulated.
32 devices in a mesh: term: 2 (over x), sector: 16 (over z, y, core).
Axes of the slice: x: 2, y: 2, z: 4, core: 2. Of those that a mesh axis runs over, the one named last changes fastest.
Arguments:
- psi_start: bfloat16 [128, 256, 256], P('sector'), may hold values from -6 to 6
- left_env: bfloat16 [6, 128, 256, 256], P('term', 'sector')
- right_env: bfloat16 [6, 128, 256, 256], P('term', 'sector')
- connect: int32 [6, 128], P('term', 'sector'), may hold values from 0 to 127, as said below
- sector_dims: int32 [2, 128], P(None, 'sector'), may hold values from 64 to 256
- precond: bfloat16 [128, 256, 256], P('sector'), may hold values from 0.5 to 4
Outputs:
- projected: float32 [3, 3], replicated
- last_vector: float32 [128, 256, 256], P('sector', 'term')
- new_env: bfloat16 [6, 128, 256, 256], P('term', 'sector')
Inputs may be any that keep to these rules, and one draw needn't show every extreme that they name: connect[t, s] differs from s by at most 8.
All inputs are finite; a program needn't handle non-finite values.
Results may differ from a plain program's by a relative error of at most 0.012.
Values may be sent and summed in bfloat16 or wider, within the bound.
A program may use at most 128 MiB of HBM per device.

v0:
```python
import jax
import jax.numpy as jnp
from jax import lax
from jax.sharding import PartitionSpec as P

epsilon = 1e-06


def with_halo(block, sides, width):
    for axis, dim in sides:
        count = lax.axis_size(axis)
        forward = [(i, i + 1) for i in range(count - 1)]
        backward = [(target, source) for source, target in forward]
        low = lax.ppermute(
            lax.slice_in_dim(block, block.shape[dim] - width, None, axis=dim), axis, forward
        )
        high = lax.ppermute(lax.slice_in_dim(block, 0, width, axis=dim), axis, backward)
        block = jnp.concatenate([low, block, high], axis=dim)
    return block


def on_device(psi_start, left_env, right_env, connect, sector_dims, precond):
    blocks = psi_start.shape[0]
    width = psi_start.shape[1]
    devices = lax.axis_size("sector")
    pieces = lax.axis_size("term")
    terms_here = left_env.shape[0]
    entries = float(blocks * devices * width * width)
    local_source = connect - (lax.axis_index("sector") * blocks - blocks)
    share = width // pieces
    share_start = lax.axis_index("term") * share
    row_ids = lax.broadcasted_iota(jnp.int32, (blocks, width, width), 1)
    col_ids = lax.broadcasted_iota(jnp.int32, (blocks, width, width), 2)
    keep = (row_ids < sector_dims[0][:, None, None]) & (col_ids < sector_dims[1][:, None, None])
    mask = keep.astype(jnp.float32)
    start_rows = psi_start.astype(jnp.float32) * mask
    divisor = precond.astype(jnp.float32)

    def totals(values):
        stacked = jnp.stack(values)
        summed = lax.psum(stacked, "sector")
        return summed / entries

    norm_start = totals([jnp.sum(start_rows * start_rows)])[0]
    basis = [start_rows / jnp.sqrt(norm_start + epsilon)]
    sigmas = []
    env_list = []
    for which in range(3):
        vector_b = basis[which].astype(jnp.bfloat16)
        extended = with_halo(vector_b, (("sector", 0),), blocks)
        with_env = which == 2
        total = jnp.zeros((blocks, width, width), jnp.float32)
        own_blocks = extended[blocks : 2 * blocks]
        envs = []
        for apply_which in range(terms_here):
            source = jnp.take(extended, local_source[apply_which], axis=0)
            half = jnp.einsum(
                "sij,sjk->sik", left_env[apply_which], source, preferred_element_type=jnp.float32
            ).astype(jnp.bfloat16)
            total = total + jnp.einsum(
                "sik,slk->sil", half, right_env[apply_which], preferred_element_type=jnp.float32
            )
            if with_env:
                env_one = jnp.einsum(
                    "sji,sjk->sik", own_blocks, half, preferred_element_type=jnp.float32
                ) * width ** (-0.5)
                envs.append(env_one.astype(jnp.bfloat16))
        sigma = lax.psum(total, "term")
        sigma, env_list = (sigma * mask, envs)
        sigmas.append(sigma)
        if which < 2:
            theta = totals([jnp.sum(basis[which] * sigma)])[0]
            corr = (sigma - theta * basis[which]) / divisor
            correlations = totals([jnp.sum(member * corr) for member in basis])
            for position in range(len(basis)):
                corr = corr - correlations[position] * basis[position]
            length = totals([jnp.sum(corr * corr)])[0]
            basis.append(corr / jnp.sqrt(length + epsilon))
    products = totals([jnp.sum(basis[row] * sigmas[col]) for row in range(3) for col in range(3)])
    projected = products.reshape(3, 3)
    last_vector = lax.dynamic_slice_in_dim(basis[2], share_start, share, 1)
    return (projected, last_vector, jnp.stack(env_list))


def solution(mesh):
    placed = (
        P("sector", None, None),
        P("term", "sector", None, None),
        P("term", "sector", None, None),
        P("term", "sector"),
        P(None, "sector"),
        P("sector", None, None),
    )
    return jax.shard_map(
        on_device,
        mesh=mesh,
        in_specs=placed,
        out_specs=(P(), P("sector", "term", None), P("term", "sector", None, None)),
        check_vma=False,
    )
```

profile of v0, /device:TPU:0, one launch (start us, length us, event | category | flops | bytes accessed | tf_op | source)
XLA Modules:
  0.0 646.5 jit_solution(17308843335064194327)
XLA Ops:
  7.2 0.8 slice_bitcast_fusion.1
  8.0 2.4 multiply_reduce_fusion.14
  10.4 35.6 %psum.77 = f32[1]{0:T(128)} all-reduce(f32[1]{0:T(128)} %bitcast.2), channel_id=1, replica_groups=mesh['term'=2,'sector'=16] {'sector'}, use_global_device_ids=true, to_apply=%region_1.0 | all-reduce | flops 1 | bytes 8 | tf_op jit(solution)/shard_map/psum | solution.py:41
  46.7 1.8 fusion.119
  48.5 1.4 collective-permute-start
  49.9 1.3 collective-permute-start.1
  51.2 0.8 collective-permute-done
  52.1 1.0 copy-done.15
  53.0 1.5 collective-permute-done.1
  54.5 2.0 pad_maximum_fusion
  56.6 1.6 gather_fusion.1
  58.2 1.6 gather_fusion
  59.7 1.6 gather_fusion.2
  61.3 4.2 fusion.3
  65.5 3.7 fusion.2
  69.2 5.0 add_add_fusion.2
  74.3 79.1 %all-reduce.4.cloned.1.call-done = f32[8,256,256]{2,1,0:T(8,128)} async-done(((f32[8,256,256]{2,1,0:T(8,128)}), f32[8,256,256]{2,1,0:T(8,128)}) %all-reduce.4.cloned.1.call-update) | async-done | bytes 2097168 | tf_op jit(solution)/shard_map/psum | solution.py:68
  153.4 3.0 multiply_reduce_fusion.13
  156.5 33.6 %psum.79 = f32[1]{0:T(128)} all-reduce(f32[1]{0:T(128)} %bitcast.13), channel_id=1, replica_groups=mesh['term'=2,'sector'=16] {'sector'}, use_global_device_ids=true, to_apply=%region_4.6 | all-reduce | flops 1 | bytes 8 | tf_op jit(solution)/shard_map/psum | solution.py:41
  190.8 2.8 multiply_reduce_fusion.12
  193.6 30.1 %psum.80 = f32[1]{0:T(128)} all-reduce(f32[1]{0:T(128)} %bitcast.15), channel_id=1, replica_groups=mesh['term'=2,'sector'=16] {'sector'}, use_global_device_ids=true, to_apply=%region_6.8 | all-reduce | flops 1 | bytes 8 | tf_op jit(solution)/shard_map/psum | solution.py:41
  224.3 3.6 multiply_reduce_fusion.11
  227.9 30.1 %psum.81 = f32[1]{0:T(128)} all-reduce(f32[1]{0:T(128)} %bitcast.17), channel_id=1, replica_groups=mesh['term'=2,'sector'=16] {'sector'}, use_global_device_ids=true, to_apply=%region_8.10 | all-reduce | flops 1 | bytes 8 | tf_op jit(solution)/shard_map/psum | solution.py:41
  258.9 1.8 collective-permute-start.2
  260.8 1.3 collective-permute-start.3
  262.1 0.9 collective-permute-done.2
  263.0 2.4 collective-permute-done.3
  265.3 1.8 pad_maximum_fusion.1
  267.2 3.5 gather_fusion.4
  270.6 3.5 gather_fusion.3
  274.1 3.5 gather_fusion.5
  277.6 4.0 fusion.5
  281.6 4.0 fusion.4
  285.6 5.3 add_add_fusion.1
  291.2 79.4 %all-reduce.6.cloned.1.call-done = f32[8,256,256]{2,1,0:T(8,128)} async-done(((f32[8,256,256]{2,1,0:T(8,128)}), f32[8,256,256]{2,1,0:T(8,128)}) %all-reduce.6.cloned.1.call-update) | async-done | bytes 2097168 | tf_op jit(solution)/shard_map/psum | solution.py:68
  370.5 2.9 multiply_reduce_fusion.9
  373.4 33.6 %psum.83 = f32[1]{0:T(128)} all-reduce(f32[1]{0:T(128)} %bitcast.20), channel_id=1, replica_groups=mesh['term'=2,'sector'=16] {'sector'}, use_global_device_ids=true, to_apply=%region_12.14 | all-reduce | flops 1 | bytes 8 | tf_op jit(solution)/shard_map/psum | solution.py:41
  407.7 3.9 multiply_reduce_fusion.8
  411.6 1.3 pad_maximum_fusion.4
  413.0 29.5 %psum.84 = f32[2]{0:T(128)S(1)} all-reduce(f32[2]{0:T(128)S(1)} %pad_maximum_fusion.4), channel_id=1, replica_groups=mesh['term'=2,'sector'=16] {'sector'}, use_global_device_ids=true, to_apply=%region_15.17 | all-reduce | flops 2 | bytes 16 | tf_op jit(solution)/shard_map/psum | solution.py:41
  443.1 6.4 multiply_reduce_fusion.6
  449.5 30.1 %psum.85 = f32[1]{0:T(128)} all-reduce(f32[1]{0:T(128)} %bitcast.26), channel_id=1, replica_groups=mesh['term'=2,'sector'=16] {'sector'}, use_global_device_ids=true, to_apply=%region_17.19 | all-reduce | flops 1 | bytes 8 | tf_op jit(solution)/shard_map/psum | solution.py:41
  480.3 3.2 fusion.121
  483.5 1.8 collective-permute-start.4
  485.3 1.3 collective-permute-start.5
  486.6 0.9 collective-permute-done.4
  487.5 2.4 collective-permute-done.5
  489.9 1.8 pad_maximum_fusion.2
  491.7 3.5 gather_fusion.6
  495.2 3.5 gather_fusion.7
  498.7 3.5 gather_fusion.8
  502.2 2.3 convolution_convert_fusion.8
  504.7 2.2 convolution_convert_fusion.7
  507.5 1.7 copy-done.5
  510.2 1.9 add_add_fusion
  512.2 2.4 constant_dynamic-slice_fusion
  514.6 1.6 fusion.6
  516.2 1.5 fusion.7
  517.7 1.5 fusion.8
  519.2 72.6 %all-reduce.8.cloned.1.call-done = f32[8,256,256]{2,1,0:T(8,128)} async-done(((f32[8,256,256]{2,1,0:T(8,128)}), f32[8,256,256]{2,1,0:T(8,128)}) %all-reduce.8.cloned.1.call-update) | async-done | bytes 2097168 | tf_op jit(solution)/shard_map/psum | solution.py:68
  591.7 4.9 multiply_reduce_fusion
  596.6 5.8 stack.81
  602.4 3.9 pad_maximum_fusion.3
  606.3 33.0 %psum.87 = f32[9]{0:T(128)S(1)} all-reduce(f32[9]{0:T(128)S(1)} %stack.81), channel_id=1, replica_groups=mesh['term'=2,'sector'=16] {'sector'}, use_global_device_ids=true, to_apply=%region_25.27 | all-reduce | flops 9 | bytes 72 | tf_op jit(solution)/shard_map/psum | solution.py:41
  (50 shorter events, 3.7 us)
Async XLA Ops:
  7.2 44.0 %copy-start.16 = (s32[3,8]{1,0:T(4,128)S(1)}, s32[3,8]{1,0:T(4,128)}, u32[]{:S(2)}) copy-start(s32[3,8]{1,0:T(4,128)} %param.11) | copy-start | bytes 292
  7.2 146.2 %all-reduce.4.cloned.1.call-start = ((), (), s32[]{:S(2)}) async-start(), calls=%async_computation | async-start | bytes 4194304 | tf_op jit(solution)/shard_map/psum | solution.py:68
  48.5 3.6 copy-start.10
  48.5 3.6 collective-permute-start
  49.9 4.7 collective-permute-start.1
  52.1 1.0 copy-start.15
  61.3 4.2 copy-start.4
  74.2 79.2 %copy-start = (bf16[8,256,256]{2,1,0:T(8,128)(2,1)S(1)}, bf16[8,256,256]{2,1,0:T(8,128)(2,1)}, u32[]{:S(2)}) copy-start(bf16[8,256,256]{2,1,0:T(8,128)(2,1)} %param.8) | copy-start | bytes 3145732
  74.2 296.3 %all-reduce.6.cloned.1.call-start = ((), (), s32[]{:S(2)}) async-start(), calls=%async_computation.1 | async-start | bytes 4194304 | tf_op jit(solution)/shard_map/psum | solution.py:68
  153.4 37.3 %copy-start.1 = (f32[8,256,256]{2,1,0:T(8,128)S(1)}, f32[8,256,256]{2,1,0:T(8,128)}, u32[]{:S(2)}) copy-start(f32[8,256,256]{2,1,0:T(8,128)} %all-reduce.4.cloned.1.call-done) | copy-start | bytes 6291460
  258.9 4.0 collective-permute-start.2
  260.8 4.6 collective-permute-start.3
  290.9 300.8 %all-reduce.8.cloned.1.call-start = ((), (), s32[]{:S(2)}) async-start(), calls=%async_computation.2 | async-start | bytes 4194304 | tf_op jit(solution)/shard_map/psum | solution.py:68
  483.5 6.4 copy-start.2
  483.5 4.0 collective-permute-start.4
  485.3 4.6 collective-permute-start.5
  502.2 2.5 copy-start.13
  504.7 5.0 copy-start.6
  504.7 2.2 copy-start.14
  506.9 2.8 copy-start.8
  506.9 2.3 copy-start.5
  509.2 1.0 copy-start.11
  512.1 2.4 copy-start.3
  512.2 2.4 copy-start.7
  514.6 1.6 copy-start.9
  516.2 1.5 copy-start.12
Sparse Core Ops, SparseCore 0:
  74.4 79.0 all-reduce.3
  291.0 79.4 all-reduce.5
  512.3 79.4 all-reduce.7
where the time goes:
time: 648 us; the launch traced here: 646 us
  blocking collectives  256 us (40%)
  waiting for transfers between devices  240 us (37%)
  other arithmetic  46.1 us (7%)
  local copies, waits for them, and re-layouts  38.9 us (6%)
  matrix products  38.6 us (6%)
  between operations  18 us (3%)
  starting transfers between devices  9.19 us (1%)
    psum x8, blocking collectives, totals(): summed = lax.psum(stacked, 'sector')  256 us
    psum x3, waiting for transfers between devices, on_device(): sigma = lax.psum(total, 'term')  231 us
    dot_general x9, matrix products, on_device(): jnp.einsum('sik,slk->sil', half, right_env[apply_which], preferred_elemen...  29 us
    gather x9, local copies, waits for them, and re-layouts, on_device(): source = jnp.take(extended, local_source[apply_which], axis=0)  25.7 us
  transfers between devices with their start and end apart: 9, of which 9 were waited for; matrix products, arithmetic and copies ran while one was open for 1% of the time, Pallas kernels for 0%

commit v1 on v0

--- a/solution.py
+++ b/solution.py
@@ -38,7 +38,7 @@
 
     def totals(values):
         stacked = jnp.stack(values)
-        summed = lax.psum(stacked, "sector")
+        summed = jnp.sum(lax.all_gather(stacked, "sector"), axis=0)
         return summed / entries
 
     norm_start = totals([jnp.sum(start_rows * start_rows)])[0]

time: 648 us -> 656 us (1.012)
  local copies, waits for them, and re-layouts: 38.9 us -> 53.1 us
    psum x8 -> x0, blocking collectives: 256 us -> none  [totals(): summed = lax.psum(stacked, 'sector')]
    unnamed x0 -> x8, blocking collectives: none -> 252 us
    unnamed x34 -> x44, local copies, waits for them, and re-layouts: 2.96 us -> 12.7 us
where the time goes in v1:
time: 656 us; the launch traced here: 654 us
  blocking collectives  252 us (38%)
  waiting for transfers between devices  239 us (36%)
  local copies, waits for them, and re-layouts  53.1 us (8%)
  other arithmetic  47.7 us (7%)
  matrix products  34 us (5%)
  between operations  19.2 us (3%)
  starting transfers between devices  9.41 us (1%)
    unnamed x8, blocking collectives  252 us
    psum x3, waiting for transfers between devices, on_device(): sigma = lax.psum(total, 'term')  229 us
    gather x9, local copies, waits for them, and re-layouts, on_device(): source = jnp.take(extended, local_source[apply_which], axis=0)  30.4 us
    dot_general x9, matrix products, on_device(): jnp.einsum('sik,slk->sil', half, right_env[apply_which], preferred_elemen...  27.5 us
  transfers between devices with their start and end apart: 9, of which 9 were waited for; matrix products, arithmetic and copies ran while one was open for 1% of the time, Pallas kernels for 0%

profile of v1, /device:TPU:0, one launch (start us, length us, event | category | flops | bytes accessed | tf_op | source)
XLA Modules:
  0.0 654.1 jit_solution(16749817365554523841)
XLA Ops:
  8.0 1.2 dynamic-slice
  9.2 2.4 multiply_reduce_fusion.14
  11.7 1.3 dynamic-update-slice
  13.0 34.9 %all-reduce = f32[16]{0:T(128)S(1)} all-reduce(f32[16]{0:T(128)S(1)} %dynamic-update-slice), channel_id=1, replica_groups=mesh['term'=2,'sector'=16] {'sector'}, use_global_device_ids=true, to_apply=%add | all-reduce | flops 16 | bytes 128
  49.2 1.8 fusion.119
  51.0 1.4 collective-permute-start
  52.4 1.3 collective-permute-start.1
  53.8 0.8 collective-permute-done
  54.6 2.4 collective-permute-done.1
  56.9 1.8 pad_maximum_fusion
  58.8 3.5 gather_fusion.1
  62.3 3.5 gather_fusion
  65.7 2.5 gather_fusion.2
  68.2 2.7 fusion.3
  70.9 4.0 fusion.2
  75.0 4.4 add_add_fusion.2
  79.5 78.3 %all-reduce.12.cloned.1.call-done = f32[8,256,256]{2,1,0:T(8,128)} async-done(((f32[8,256,256]{2,1,0:T(8,128)}), f32[8,256,256]{2,1,0:T(8,128)}) %all-reduce.12.cloned.1.call-update) | async-done | bytes 2097168 | tf_op jit(solution)/shard_map/psum | solution.py:68
  157.7 3.0 multiply_reduce_fusion.13
  160.8 1.3 dynamic-update-slice.1
  162.1 33.0 %all-reduce.1 = f32[16]{0:T(128)S(1)} all-reduce(f32[16]{0:T(128)S(1)} %dynamic-update-slice.1), channel_id=1, replica_groups=mesh['term'=2,'sector'=16] {'sector'}, use_global_device_ids=true, to_apply=%add.1 | all-reduce | flops 16 | bytes 128
  196.3 2.8 multiply_reduce_fusion.12
  199.1 1.3 dynamic-update-slice.2
  200.5 29.5 %all-reduce.2 = f32[16]{0:T(128)S(1)} all-reduce(f32[16]{0:T(128)S(1)} %dynamic-update-slice.2), channel_id=1, replica_groups=mesh['term'=2,'sector'=16] {'sector'}, use_global_device_ids=true, to_apply=%add.2 | all-reduce | flops 16 | bytes 128
  231.2 3.6 multiply_reduce_fusion.11
  234.8 1.3 dynamic-update-slice.3
  236.1 29.5 %all-reduce.3 = f32[16]{0:T(128)S(1)} all-reduce(f32[16]{0:T(128)S(1)} %dynamic-update-slice.3), channel_id=1, replica_groups=mesh['term'=2,'sector'=16] {'sector'}, use_global_device_ids=true, to_apply=%add.3 | all-reduce | flops 16 | bytes 128
  267.1 1.8 collective-permute-start.2
  268.9 1.5 collective-permute-start.3
  271.1 2.4 collective-permute-done.3
  273.5 1.8 pad_maximum_fusion.1
  275.3 3.5 gather_fusion.4
  278.8 3.5 gather_fusion.3
  282.3 3.5 gather_fusion.5
  285.8 4.0 fusion.5
  289.8 4.0 fusion.4
  293.8 5.4 add_add_fusion.1
  299.2 79.6 %all-reduce.14.cloned.1.call-done = f32[8,256,256]{2,1,0:T(8,128)} async-done(((f32[8,256,256]{2,1,0:T(8,128)}), f32[8,256,256]{2,1,0:T(8,128)}) %all-reduce.14.cloned.1.call-update) | async-done | bytes 2097168 | tf_op jit(solution)/shard_map/psum | solution.py:68
  378.8 2.8 multiply_reduce_fusion.9
  381.6 1.2 dynamic-update-slice.4
  383.4 33.0 %all-reduce.4 = f32[16]{0:T(128)S(1)} all-reduce(f32[16]{0:T(128)S(1)} %dynamic-update-slice.4), channel_id=1, replica_groups=mesh['term'=2,'sector'=16] {'sector'}, use_global_device_ids=true, to_apply=%add.4 | all-reduce | flops 16 | bytes 128
  417.7 3.8 multiply_reduce_fusion.8
  421.5 1.5 maximum_dynamic-update-slice_fusion
  423.0 29.5 %all-reduce.5 = f32[32]{0:T(128)S(1)} all-reduce(f32[32]{0:T(128)S(1)} %maximum_dynamic-update-slice_fusion), channel_id=2, replica_groups=mesh['term'=2,'sector'=16] {'sector'}, use_global_device_ids=true, to_apply=%add.5 | all-reduce | flops 32 | bytes 256
  453.2 6.4 multiply_reduce_fusion.6
  459.6 1.3 dynamic-update-slice.6
  460.9 29.5 %all-reduce.6 = f32[16]{0:T(128)S(1)} all-reduce(f32[16]{0:T(128)S(1)} %dynamic-update-slice.6), channel_id=1, replica_groups=mesh['term'=2,'sector'=16] {'sector'}, use_global_device_ids=true, to_apply=%add.6 | all-reduce | flops 16 | bytes 128
  491.6 3.2 fusion.121
  494.8 1.8 collective-permute-start.4
  496.7 1.5 collective-permute-start.5
  498.9 2.4 collective-permute-done.5
  501.2 1.8 pad_maximum_fusion.2
  503.1 3.5 gather_fusion.6
  506.5 3.5 gather_fusion.7
  510.0 3.5 gather_fusion.8
  513.5 2.3 convolution_convert_fusion.2
  516.0 2.2 convolution_convert_fusion.1
  518.9 1.7 copy-done.4
  521.6 1.9 add_add_fusion
  524.2 2.4 constant_dynamic-slice_fusion
  529.6 2.0 pad_maximum_fusion.3
  531.6 71.6 %all-reduce.16.cloned.1.call-done = f32[8,256,256]{2,1,0:T(8,128)} async-done(((f32[8,256,256]{2,1,0:T(8,128)}), f32[8,256,256]{2,1,0:T(8,128)}) %all-reduce.16.cloned.1.call-update) | async-done | bytes 2097168 | tf_op jit(solution)/shard_map/psum | solution.py:68
  603.2 4.9 multiply_reduce_fusion
  608.1 5.5 stack.63
  613.8 33.0 %all-reduce.7 = f32[144]{0:T(256)S(1)} all-reduce(f32[144]{0:T(256)S(1)} %dynamic-update-slice.7), channel_id=3, replica_groups=mesh['term'=2,'sector'=16] {'sector'}, use_global_device_ids=true, to_apply=%add.7 | all-reduce | flops 144 | bytes 1152
  (70 shorter events, 12.7 us)
Async XLA Ops:
  7.2 46.5 %copy-start.13 = (s32[3,8]{1,0:T(4,128)S(1)}, s32[3,8]{1,0:T(4,128)}, u32[]{:S(2)}) copy-start(s32[3,8]{1,0:T(4,128)} %param.11) | copy-start | bytes 292
  7.2 150.6 %all-reduce.12.cloned.1.call-start = ((), (), s32[]{:S(2)}) async-start(), calls=%async_computation | async-start | bytes 4194304 | tf_op jit(solution)/shard_map/psum | solution.py:68
  51.0 3.6 collective-permute-start
  52.4 4.6 collective-permute-start.1
  79.4 78.4 %copy-start = (bf16[8,256,256]{2,1,0:T(8,128)(2,1)S(1)}, bf16[8,256,256]{2,1,0:T(8,128)(2,1)}, u32[]{:S(2)}) copy-start(bf16[8,256,256]{2,1,0:T(8,128)(2,1)} %param.8) | copy-start | bytes 3145732
  79.4 299.4 %all-reduce.14.cloned.1.call-start = ((), (), s32[]{:S(2)}) async-start(), calls=%async_computation.1 | async-start | bytes 4194304 | tf_op jit(solution)/shard_map/psum | solution.py:68
  157.7 38.6 %copy-start.1 = (f32[8,256,256]{2,1,0:T(8,128)S(1)}, f32[8,256,256]{2,1,0:T(8,128)}, u32[]{:S(2)}) copy-start(f32[8,256,256]{2,1,0:T(8,128)} %all-reduce.12.cloned.1.call-done) | copy-start | bytes 6291460
  267.1 4.0 collective-permute-start.2
  268.9 4.6 collective-permute-start.3
  299.2 304.0 %all-reduce.16.cloned.1.call-start = ((), (), s32[]{:S(2)}) async-start(), calls=%async_computation.2 | async-start | bytes 4194304 | tf_op jit(solution)/shard_map/psum | solution.py:68
  494.8 6.4 copy-start.2
  494.8 4.0 collective-permute-start.4
  496.7 4.6 collective-permute-start.5
  513.5 2.5 copy-start.11
  516.0 5.0 copy-start.5
  516.0 2.2 copy-start.12
  518.3 2.8 copy-start.7
  518.3 2.3 copy-start.4
  520.6 1.0 copy-start.9
  524.1 2.4 copy-start.3
  524.1 2.4 copy-start.6
  526.6 1.2 copy-start.8
  527.8 1.2 copy-start.10
Sparse Core Ops, SparseCore 0:
  79.5 78.1 all-reduce.11
  299.3 79.4 all-reduce.13
  523.7 79.4 all-reduce.15
